TPU v7x, 32 devices: a whole 2x2x4 slice. The times are simulated.
32 devices in a mesh: groups: 2 (over y), row: 4 (over z), col: 2 (over x), rep: 2 (over core).
Axes of the slice: x: 2, y: 2, z: 4, core: 2. Of those that a mesh axis runs over, the one named last changes fastest.
Arguments:
- kernel: float32 [32768, 16384], P(('groups', 'row'), ('col', 'rep')), parts along dimension 0, may hold values from 0 to 2, as said below
- source: float32 [64, 16384], P('groups', 'row'), parts along dimension 0, may hold values from 0.5 to 2, as said below
- target: float32 [64, 16384], P('groups', ('col', 'rep')), parts along dimension 0, may hold values from 0.5 to 2, as said below
Outputs:
- left_scale: float32 [64, 16384], P('groups', 'row'), parts along dimension 0
- right_scale: float32 [64, 16384], P('groups', ('col', 'rep')), parts along dimension 0
- errors: float32 [6, 32], P('groups'), parts along dimension 0
There are 2 independent parts, one for each index of `groups`. A program takes and returns all parts, laid end to end along the dimension named above; each array names one. Nothing has to cross between parts.
Inputs may be any that keep to these rules, and one draw needn't show every extreme that they name: `kernel`: every entry is positive. `source`: every entry is positive. `target`: every entry is positive.
All inputs are finite; a program needn't handle non-finite values.
Results may differ from a plain program's by a relative error of at most 0.0001.
Values sent between devices are 32-bit elements; how exact they have to be, the bound alone decides.
A program may use at most 128 MiB of HBM per device.

v0:
```python
import jax
import jax.numpy as jnp
from jax import lax
from jax.sharding import PartitionSpec as P

N = 16384
ITERS = 3


def local(kernel, source, target):
    columns = kernel.shape[1]
    right_scale = jnp.ones(target.shape, jnp.float32)
    left_scale = source
    share = columns // lax.axis_size("row")
    offset = lax.axis_index("row") * share
    errors = []
    for step in range(ITERS):
        partial_value = lax.dot_general(
            right_scale, kernel, (((1,), (1,)), ((), ())), precision=lax.Precision.HIGHEST
        )
        left_scale = source / lax.psum(partial_value, ("col", "rep"))
        back = jnp.dot(left_scale, kernel, precision=lax.Precision.HIGHEST)
        old_piece = lax.dynamic_slice_in_dim(right_scale, offset, share, 1)
        target_piece = lax.dynamic_slice_in_dim(target, offset, share, 1)
        total_piece = lax.psum_scatter(back, "row", scatter_dimension=1, tiled=True)
        right_scale = lax.all_gather(target_piece / total_piece, "row", axis=1, tiled=True)
        term = jnp.sum(jnp.abs(old_piece * total_piece - target_piece), axis=1) / N
        errors.append(lax.psum(term, ("row", "col", "rep")))
    stacked = jnp.stack(errors)
    return (left_scale, right_scale, stacked)


def solution(mesh):
    return jax.shard_map(
        local,
        mesh=mesh,
        in_specs=(
            P(("groups", "row"), ("col", "rep")),
            P("groups", "row"),
            P("groups", ("col", "rep")),
        ),
        out_specs=(P("groups", "row"), P("groups", ("col", "rep")), P("groups", None)),
        check_vma=False,
    )
```

profile of v0, /device:TPU:0, one launch (start us, length us, event | category | flops | bytes accessed | tf_op | source)
XLA Modules:
  0.0 597.1 jit_solution(12538912805392526422)
XLA Ops:
  7.2 0.0 copy-start
  7.2 0.0 all-reduce.5.cloned.1.call-start
  7.2 66.4 %fusion.4 = f32[32,4096]{1,0:T(8,128)} fusion(f32[4096,4096]{1,0:T(8,128)} %param.3), kind=kOutput, calls=%fused_computation.4 | convolution fusion | flops 6442450944 | bytes 67633152 | tf_op jit(solution)/shard_map/dot_general | solution.py:18
  73.7 0.0 copy-start.4
  73.7 0.0 all-reduce.5.cloned.1.call-update
  73.7 0.3 reduce-scatter.4.cloned.1.call-start
  74.0 36.0 %all-reduce.5.cloned.1.call-done = f32[32,4096]{1,0:T(8,128)} async-done(((f32[32,4096]{1,0:T(8,128)}), f32[32,4096]{1,0:T(8,128)}) %all-reduce.5.cloned.1.call-update) | async-done | bytes 524304 | tf_op jit(solution)/shard_map/psum | solution.py:21
  110.0 0.0 copy-done
  110.0 44.8 %fusion.2 = f32[32,4096]{1,0:T(8,128)} fusion(f32[4096,4096]{1,0:T(8,128)} %param.3, f32[32,4096]{1,0:T(8,128)S(1)} %copy-done, f32[32,4096]{1,0:T(8,128)} %all-reduce.5.cloned.1.call-done), kind=kOutput, calls=%fused_computation.2 | convolution fusion | flops 6442582016 | bytes 68681728 | tf_op jit(solution)/shard_map/dot_general | solution.py:22
  154.8 0.0 reduce-scatter.4.cloned.1.call-update
  154.9 0.0 all-reduce.7.cloned.1.call-start
  154.9 22.1 %reduce-scatter.4.cloned.1.call-done = f32[32,1024]{1,0:T(8,128)} async-done(((f32[32,4096]{1,0:T(8,128)}), f32[32,1024]{1,0:T(8,128)}) %reduce-scatter.4.cloned.1.call-update) | async-done | bytes 131088 | tf_op jit(solution)/shard_map/reduce_scatter | solution.py:25
  177.0 0.0 copy-done.4
  177.0 0.9 dynamic-slice_divide_fusion.2
  177.9 15.7 %all_gather.9 = f32[32,4096]{1,0:T(8,128)S(1)} all-gather(f32[32,1024]{1,0:T(8,128)S(1)} %dynamic-slice_divide_fusion.2), channel_id=1, replica_groups=mesh['groups'=2,'row'=4,'col'=2,'rep'=2] {'row'}, dimensions={1}, use_global_device_ids=true | all-gather | bytes 655360 | tf_op jit(solution)/shard_map/all_gather | solution.py:26
  193.7 66.5 %fusion.7 = f32[32,4096]{1,0:T(8,128)} fusion(f32[32,4096]{1,0:T(8,128)S(1)} %all_gather.9, f32[4096,4096]{1,0:T(8,128)} %param.3), kind=kOutput, calls=%fused_computation.17 | convolution fusion | flops 6442450944 | bytes 68157440 | tf_op jit(solution)/shard_map/dot_general | solution.py:18
  260.2 0.0 all-reduce.7.cloned.1.call-update
  260.2 0.2 reduce-scatter.6.cloned.1.call-start
  260.4 31.8 %all-reduce.7.cloned.1.call-done = f32[32,4096]{1,0:T(8,128)} async-done(((f32[32,4096]{1,0:T(8,128)}), f32[32,4096]{1,0:T(8,128)}) %all-reduce.7.cloned.1.call-update) | async-done | bytes 524304 | tf_op jit(solution)/shard_map/psum | solution.py:21
  292.2 44.8 %fusion = f32[32,4096]{1,0:T(8,128)} fusion(f32[4096,4096]{1,0:T(8,128)} %param.3, f32[32,4096]{1,0:T(8,128)S(1)} %copy-done, f32[32,4096]{1,0:T(8,128)} %all-reduce.7.cloned.1.call-done), kind=kOutput, calls=%fused_computation | convolution fusion | flops 6442582016 | bytes 68681728 | tf_op jit(solution)/shard_map/dot_general | solution.py:22
  337.0 0.0 reduce-scatter.6.cloned.1.call-update
  337.0 0.0 all-reduce.9.cloned.1.call-start
  337.1 22.0 %reduce-scatter.6.cloned.1.call-done = f32[32,1024]{1,0:T(8,128)} async-done(((f32[32,4096]{1,0:T(8,128)}), f32[32,1024]{1,0:T(8,128)}) %reduce-scatter.6.cloned.1.call-update) | async-done | bytes 131088 | tf_op jit(solution)/shard_map/reduce_scatter | solution.py:25
  359.1 0.9 dynamic-slice_divide_fusion.1
  360.0 15.7 %all_gather.10 = f32[32,4096]{1,0:T(8,128)S(1)} all-gather(f32[32,1024]{1,0:T(8,128)S(1)} %dynamic-slice_divide_fusion.1), channel_id=1, replica_groups=mesh['groups'=2,'row'=4,'col'=2,'rep'=2] {'row'}, dimensions={1}, use_global_device_ids=true | all-gather | bytes 655360 | tf_op jit(solution)/shard_map/all_gather | solution.py:26
  375.7 66.5 %fusion.8 = f32[32,4096]{1,0:T(8,128)} fusion(f32[32,4096]{1,0:T(8,128)S(1)} %all_gather.10, f32[4096,4096]{1,0:T(8,128)} %param.3), kind=kOutput, calls=%fused_computation.18 | convolution fusion | flops 6442450944 | bytes 68157440 | tf_op jit(solution)/shard_map/dot_general | solution.py:18
  442.2 0.0 copy-start.2
  442.2 0.0 copy-start.3
  442.2 0.0 all-reduce.9.cloned.1.call-update
  442.2 0.3 reduce-scatter.8.cloned.1.call-start
  442.5 31.6 %all-reduce.9.cloned.1.call-done = f32[32,4096]{1,0:T(8,128)} async-done(((f32[32,4096]{1,0:T(8,128)}), f32[32,4096]{1,0:T(8,128)}) %all-reduce.9.cloned.1.call-update) | async-done | bytes 524304 | tf_op jit(solution)/shard_map/psum | solution.py:21
  474.2 1.1 div.31
  475.3 0.0 copy-start.1
  475.3 45.0 %fusion.9 = f32[32,4096]{1,0:T(8,128)} fusion(f32[32,4096]{1,0:T(8,128)S(1)} %div.31, f32[4096,4096]{1,0:T(8,128)} %param.3), kind=kOutput, calls=%fused_computation.19 | convolution fusion | flops 6442450944 | bytes 68157440 | tf_op jit(solution)/shard_map/dot_general | solution.py:22
  520.3 0.0 reduce-scatter.8.cloned.1.call-update
  520.4 22.1 %reduce-scatter.8.cloned.1.call-done = f32[32,1024]{1,0:T(8,128)} async-done(((f32[32,4096]{1,0:T(8,128)}), f32[32,1024]{1,0:T(8,128)}) %reduce-scatter.8.cloned.1.call-update) | async-done | bytes 131088 | tf_op jit(solution)/shard_map/reduce_scatter | solution.py:25
  542.5 0.0 copy-done.2
  542.5 0.0 copy-done.3
  542.5 1.1 abs_reduce_fusion.2
  543.6 15.3 %all_gather.11 = f32[32,4096]{1,0:T(8,128)S(1)} all-gather(f32[32,1024]{1,0:T(8,128)S(1)} %get-tuple-element.9), channel_id=1, replica_groups=mesh['groups'=2,'row'=4,'col'=2,'rep'=2] {'row'}, dimensions={1}, use_global_device_ids=true | all-gather | bytes 655360 | tf_op jit(solution)/shard_map/all_gather | solution.py:26
  558.9 29.5 %all-reduce = (f32[1,32]{1,0:T(1,128)S(1)}, f32[1,32]{1,0:T(1,128)S(1)}, f32[1,32]{1,0:T(1,128)S(1)}) all-reduce(f32[1,32]{1,0:T(1,128)S(1)} %get-tuple-element.10, f32[1,32]{1,0:T(1,128)S(1)} %get-tuple-element.11, f32[1,32]{1,0:T(1,128)S(1)} %multiply_bitcast_fusion.2), channel_id=1, replica_groups=mesh['groups'=2,'row'=4,'col'=2,'rep'=2] {'row','col','rep'}, use_global_device_ids=true, to_apply=%region_11.0 | all-reduce | flops 96 | bytes 768 | tf_op jit(solution)/shard_map/psum | solution.py:28
  588.4 0.6 pad_maximum_fusion
  589.0 0.8 copy.10
  589.8 0.0 copy-done.1
  (2 shorter events, 0.0 us)
Async XLA Ops:
  7.2 102.8 %copy-start = (f32[32,4096]{1,0:T(8,128)S(1)}, f32[32,4096]{1,0:T(8,128)}, u32[]{:S(2)}) copy-start(f32[32,4096]{1,0:T(8,128)} %param.4) | copy-start | bytes 1572868
  7.2 102.8 %all-reduce.5.cloned.1.call-start = ((), (), s32[]{:S(2)}) async-start(), calls=%async_computation.3 | async-start | bytes 1048576 | tf_op jit(solution)/shard_map/psum | solution.py:21
  73.7 103.3 %copy-start.4 = (f32[32,4096]{1,0:T(8,128)S(1)}, f32[32,4096]{1,0:T(8,128)}, u32[]{:S(2)}) copy-start(f32[32,4096]{1,0:T(8,128)} %param.5) | copy-start | bytes 1572868
  73.7 103.3 %reduce-scatter.4.cloned.1.call-start = ((), (), s32[]{:S(2)}) async-start(), calls=%async_computation.4 | async-start | bytes 655360 | tf_op jit(solution)/shard_map/reduce_scatter | solution.py:25
  154.9 137.3 %all-reduce.7.cloned.1.call-start = ((), (), s32[]{:S(2)}) async-start(), calls=%async_computation.5 | async-start | bytes 1048576 | tf_op jit(solution)/shard_map/psum | solution.py:21
  260.2 98.9 %reduce-scatter.6.cloned.1.call-start = ((), (), s32[]{:S(2)}) async-start(), calls=%async_computation.6 | async-start | bytes 655360 | tf_op jit(solution)/shard_map/reduce_scatter | solution.py:25
  337.0 137.1 %all-reduce.9.cloned.1.call-start = ((), (), s32[]{:S(2)}) async-start(), calls=%async_computation.7 | async-start | bytes 1048576 | tf_op jit(solution)/shard_map/psum | solution.py:21
  442.2 100.3 %copy-start.2 = (f32[32,1024]{1,0:T(8,128)S(1)}, f32[32,1024]{1,0:T(8,128)}, u32[]{:S(2)}) copy-start(f32[32,1024]{1,0:T(8,128)} %reduce-scatter.4.cloned.1.call-done) | copy-start | bytes 393220
  442.2 100.3 %copy-start.3 = (f32[32,1024]{1,0:T(8,128)S(1)}, f32[32,1024]{1,0:T(8,128)}, u32[]{:S(2)}) copy-start(f32[32,1024]{1,0:T(8,128)} %reduce-scatter.6.cloned.1.call-done) | copy-start | bytes 393220
  442.2 100.2 %reduce-scatter.8.cloned.1.call-start = ((), (), s32[]{:S(2)}) async-start(), calls=%async_computation.8 | async-start | bytes 655360 | tf_op jit(solution)/shard_map/reduce_scatter | solution.py:25
  475.3 114.5 %copy-start.1 = (f32[32,4096]{1,0:T(8,128)}, f32[32,4096]{1,0:T(8,128)S(1)}, u32[]{:S(2)}) copy-start(f32[32,4096]{1,0:T(8,128)S(1)} %div.31) | copy-start | bytes 1572868
Sparse Core Ops, SparseCore 0:
  73.8 36.1 all-reduce.4
  155.0 21.9 reduce-scatter.3
  260.3 31.8 all-reduce.6
  337.1 21.9 reduce-scatter.5
  442.4 31.7 all-reduce.8
  520.5 21.9 reduce-scatter.7
where the time goes:
time: 606 us; the launch traced here: 597 us
  matrix products  334 us (55%)
  waiting for transfers between devices  166 us (27%)
  blocking collectives  76.2 us (13%)
  between operations  14.6 us (2%)
    dot_general x3, matrix products, local(): lax.dot_general(right_scale, kernel, (((1,), (1,)), ((), ())), precision=...  199 us
    dot_general x3, matrix products, local(): back = jnp.dot(left_scale, kernel, precision=lax.Precision.HIGHEST)  135 us
    psum x3, waiting for transfers between devices, local(): left_scale = source / lax.psum(partial_value, ('col', 'rep'))  99.4 us
    reduce_scatter x3, waiting for transfers between devices, local(): total_piece = lax.psum_scatter(back, 'row', scatter_dimension=1, tiled=True)  66.2 us
    all_gather x3, blocking collectives, local(): lax.all_gather(target_piece / total_piece, 'row', axis=1, tiled=True)  46.8 us
    psum x1, blocking collectives, local(): errors.append(lax.psum(term, ('row', 'col', 'rep')))  29.5 us
  transfers between devices with their start and end apart: 6, of which 6 were waited for; matrix products, arithmetic and copies ran while one was open for 0% of the time, Pallas kernels for 0%

commit v1 on v0

v1 whole, which is shorter than its diff:
```python
import functools

import jax
import jax.numpy as jnp
from jax import lax
from jax.experimental import pallas as pl
from jax.experimental.pallas import tpu as pltpu
from jax.sharding import PartitionSpec as P

ITERS = 3
BLOCK = 256
CHUNK = 1024
LAG = 3
MESH = pl.DeviceIdType.MESH


def split(x):
    hi = x.astype(jnp.bfloat16)
    return hi, (x - hi.astype(jnp.float32)).astype(jnp.bfloat16)


def body(R, C, k_hbm, src, tgt, u_out, v_out, e_out,
         kf, kh, kl, vhl, acc, red, rsrx, vbuf, part, rx1, rx2, eb, erx1, erx2,
         ksem, s1, r1, s2, r2, srs, rrs, sag, rag, se, re):
    rows, cols = k_hbm.shape
    pairs = src.shape[0]
    nb = rows // BLOCK
    pr = pairs // R
    ring = kh.shape[0]
    me_r = lax.axis_index("row")
    me_c = lax.axis_index("col")
    me_k = lax.axis_index("rep")
    other = 1 - me_k

    def load(b):
        b = lax.rem(b, nb)
        return pltpu.make_async_copy(
            k_hbm.at[pl.ds(pl.multiple_of(b * BLOCK, BLOCK), BLOCK), :],
            kf.at[lax.rem(b, 2)], ksem.at[lax.rem(b, 2)])

    load(0).start()
    load(1).start()

    barrier = pltpu.get_barrier_semaphore()
    pl.semaphore_signal(barrier, inc=1, device_id={"rep": other}, device_id_type=MESH)
    for k in range(1, C):
        pl.semaphore_signal(barrier, inc=1, device_id={"col": lax.rem(me_c + k, C)}, device_id_type=MESH)
    for k in range(1, R):
        pl.semaphore_signal(barrier, inc=1, device_id={"row": lax.rem(me_r + k, R)}, device_id_type=MESH)
    pl.semaphore_wait(barrier, 1 + (C - 1) + (R - 1))

    vhl[0:pairs, :] = jnp.ones((pairs, cols), jnp.bfloat16)
    vhl[pairs:, :] = jnp.zeros((pairs, cols), jnp.bfloat16)
    vbuf[0, :, :, 0:cols] = jnp.ones((R, pr, cols), jnp.float32)

    def to_rep(src_ref, dst_ref, ssem, rsem):
        return pltpu.make_async_remote_copy(
            src_ref=src_ref, dst_ref=dst_ref, send_sem=ssem, recv_sem=rsem,
            device_id={"rep": other}, device_id_type=MESH)

    def to_col(k, src_ref, dst_ref, ssem, rsem):
        return pltpu.make_async_remote_copy(
            src_ref=src_ref, dst_ref=dst_ref, send_sem=ssem, recv_sem=rsem,
            device_id={"col": lax.rem(me_c + k, C)}, device_id_type=MESH)

    def to_row(k, src_ref, dst_ref, ssem, rsem):
        return pltpu.make_async_remote_copy(
            src_ref=src_ref, dst_ref=dst_ref, send_sem=ssem, recv_sem=rsem,
            device_id={"row": lax.rem(me_r + k, R)}, device_id_type=MESH)

    def first(g):
        return to_rep(part.at[g], rx1.at[g], s1.at[g], r1.at[g])

    for t in range(ITERS):
        base = (t % 2) * nb
        acc[...] = jnp.zeros_like(acc)

        @pl.loop(0, nb + LAG)
        def _(s):
            @pl.when(s < nb)
            def _():
                slot = lax.rem(s, 2)
                hold = lax.rem(s, ring)
                load(s).wait()
                total = jnp.zeros((2 * pairs, BLOCK), jnp.float32)
                for c in range(0, cols, CHUNK):
                    hi, lo = split(kf[slot, :, c:c + CHUNK])
                    kh[hold, :, c:c + CHUNK] = hi
                    kl[hold, :, c:c + CHUNK] = lo
                    v = vhl[:, c:c + CHUNK]
                    dims = (((1,), (1,)), ((), ()))
                    total += lax.dot_general(v, hi, dims, preferred_element_type=jnp.float32)
                    total += lax.dot_general(v, lo, dims, preferred_element_type=jnp.float32)
                part[base + s] = total[:pairs] + total[pairs:]
                first(base + s).start()
                if t < ITERS - 1:
                    load(s + 2).start()
                else:
                    @pl.when(s + 2 < nb)
                    def _():
                        load(s + 2).start()

            @pl.when((s >= 1) & (s <= nb))
            def _():
                g = base + s - 1
                first(g).wait()
                rx2[g, me_c] = part[g] + rx1[g]
                for k in range(1, C):
                    to_col(k, rx2.at[g, me_c], rx2.at[g, me_c], s2.at[g, k], r2.at[g, k]).start()

            @pl.when(s >= LAG)
            def _():
                b = s - LAG
                g = base + b
                hold = lax.rem(b, ring)
                for k in range(1, C):
                    peer = lax.rem(me_c + (C - k), C)
                    to_col(k, rx2.at[g, peer], rx2.at[g, peer], s2.at[g, k], r2.at[g, k]).wait()
                kv = rx2[g, 0]
                for c in range(1, C):
                    kv += rx2[g, c]
                at = pl.ds(pl.multiple_of(b * BLOCK, BLOCK), BLOCK)
                u = src[:, at] / kv
                u_out[:, at] = u
                hi, lo = split(u)
                uhl = jnp.concatenate([hi, lo], axis=0)
                acc[...] += (jnp.dot(uhl, kh[hold], preferred_element_type=jnp.float32)
                             + jnp.dot(uhl, kl[hold], preferred_element_type=jnp.float32))

        for q in range(R):
            red[q] = acc[q * pr:(q + 1) * pr, :] + acc[pairs + q * pr:pairs + (q + 1) * pr, :]
        for k in range(1, R):
            to_row(k, red.at[lax.rem(me_r + k, R)], rsrx.at[t, me_r], srs.at[k], rrs.at[k]).start()
        total = red[me_r]
        for k in range(1, R):
            peer = lax.rem(me_r + (R - k), R)
            to_row(k, red.at[lax.rem(me_r + k, R)], rsrx.at[t, peer], srs.at[k], rrs.at[k]).wait()
            total += rsrx[t, peer]
        goal = tgt[me_r]
        diff = jnp.abs(vbuf[t, me_r, :, 0:cols] * total - goal)
        lanes = diff[:, 0:128]
        for c in range(128, cols, 128):
            lanes += diff[:, c:c + 128]
        vbuf[t + 1, me_r, :, 0:cols] = goal / total
        vbuf[t + 1, me_r, :, cols:cols + 128] = lanes
        for k in range(1, R):
            to_row(k, vbuf.at[t + 1, me_r], vbuf.at[t + 1, me_r], sag.at[k], rag.at[k]).start()
        for k in range(1, R):
            peer = lax.rem(me_r + (R - k), R)
            to_row(k, vbuf.at[t + 1, peer], vbuf.at[t + 1, peer], sag.at[k], rag.at[k]).wait()
        full = jnp.concatenate([vbuf[t + 1, q, :, 0:cols] for q in range(R)], axis=0)
        if t < ITERS - 1:
            hi, lo = split(full)
            vhl[0:pairs, :] = hi
            vhl[pairs:, :] = lo
        else:
            v_out[...] = full
        eb[t] = jnp.concatenate([vbuf[t + 1, q, :, cols:cols + 128] for q in range(R)], axis=0)

    swap = to_rep(eb, erx1, se.at[0], re.at[0])
    swap.start()
    swap.wait()
    erx2[me_c] = eb[...] + erx1[...]
    for k in range(1, C):
        to_col(k, erx2.at[me_c], erx2.at[me_c], se.at[k], re.at[k]).start()
    for k in range(1, C):
        peer = lax.rem(me_c + (C - k), C)
        to_col(k, erx2.at[peer], erx2.at[peer], se.at[k], re.at[k]).wait()
    e = erx2[0]
    for c in range(1, C):
        e += erx2[c]
    e_out[...] = e


def local(R, C, D, kernel, source, target):
    rows, cols = kernel.shape
    pairs = source.shape[0]
    pr = pairs // R
    nb = rows // BLOCK
    f32, bf16 = jnp.float32, jnp.bfloat16
    dma = pltpu.SemaphoreType.DMA
    vmem = pl.BlockSpec(memory_space=pltpu.VMEM)
    ring = LAG + 1
    u, v, e = pl.pallas_call(
        functools.partial(body, R, C),
        out_shape=(
            jax.ShapeDtypeStruct((pairs, rows), f32),
            jax.ShapeDtypeStruct((pairs, cols), f32),
            jax.ShapeDtypeStruct((ITERS, pairs, 128), f32),
        ),
        in_specs=[pl.BlockSpec(memory_space=pl.ANY), vmem, vmem],
        out_specs=(vmem, vmem, vmem),
        scratch_shapes=[
            pltpu.VMEM((2, BLOCK, cols), f32),
            pltpu.VMEM((ring, BLOCK, cols), bf16),
            pltpu.VMEM((ring, BLOCK, cols), bf16),
            pltpu.VMEM((2 * pairs, cols), bf16),
            pltpu.VMEM((2 * pairs, cols), f32),
            pltpu.VMEM((R, pr, cols), f32),
            pltpu.VMEM((ITERS, R, pr, cols), f32),
            pltpu.VMEM((ITERS + 1, R, pr, cols + 128), f32),
            pltpu.VMEM((2 * nb, pairs, BLOCK), f32),
            pltpu.VMEM((2 * nb, pairs, BLOCK), f32),
            pltpu.VMEM((2 * nb, C, pairs, BLOCK), f32),
            pltpu.VMEM((ITERS, pairs, 128), f32),
            pltpu.VMEM((ITERS, pairs, 128), f32),
            pltpu.VMEM((C, ITERS, pairs, 128), f32),
            dma((2,)),
            dma((2 * nb,)), dma((2 * nb,)),
            dma((2 * nb, C)), dma((2 * nb, C)),
            dma((R,)), dma((R,)), dma((R,)), dma((R,)),
            dma((C,)), dma((C,)),
        ],
        compiler_params=pltpu.CompilerParams(
            collective_id=0, has_side_effects=True, vmem_limit_bytes=60 << 20),
    )(kernel, source, target.reshape(R, pr, cols))
    return u, v, jnp.sum(e, axis=2) / (cols * D)


def solution(mesh):
    R, C, K = (mesh.shape[a] for a in ("row", "col", "rep"))
    return jax.shard_map(
        functools.partial(local, R, C, C * K),
        mesh=mesh,
        in_specs=(
            P(("groups", "row"), ("col", "rep")),
            P("groups", "row"),
            P("groups", ("col", "rep")),
        ),
        out_specs=(P("groups", "row"), P("groups", ("col", "rep")), P("groups", None)),
        check_vma=False,
    )
```

time: 606 us -> 215 us (0.35); the launches traced: 597 us -> 214 us
  matrix products: 334 us -> 0 us
  Pallas kernels: 0 us -> 208 us
  waiting for transfers between devices: 166 us -> 0 us
  blocking collectives: 76.2 us -> 0 us
  between operations: 14.6 us -> 0.64 us
    dot_general x6 -> x0, matrix products: 334 us -> none  [the longest x3 199 us: local(): lax.dot_general(right_scale, kernel, (((1,), (1,)), ((), ())), precision=...]
    pallas_call x0 -> x1, Pallas kernels: none -> 208 us  [local(): pl.pallas_call(functools.partial(body, R, C), out_shape=(jax.ShapeDtypeSt...]
    psum x3 -> x0, waiting for transfers between devices: 99.4 us -> none  [local(): left_scale = source / lax.psum(partial_value, ('col', 'rep'))]
    reduce_scatter x3 -> x0, waiting for transfers between devices: 66.2 us -> none  [local(): total_piece = lax.psum_scatter(back, 'row', scatter_dimension=1, tiled=True)]
    all_gather x3 -> x0, blocking collectives: 46.8 us -> none  [local(): lax.all_gather(target_piece / total_piece, 'row', axis=1, tiled=True)]
    psum x1 -> x0, blocking collectives: 29.5 us -> none  [local(): errors.append(lax.psum(term, ('row', 'col', 'rep')))]
  transfers between devices with their start and end apart: 6 -> 0, of which waited for: 6 -> 0; matrix products, arithmetic and copies ran while one was open for 0% -> 0% of each run, Pallas kernels for 0% -> 0%
where the time goes in v1:
time: 215 us; the launch traced here: 214 us
  Pallas kernels  208 us (97%)
  local copies, waits for them, and re-layouts  3.74 us (2%)
    pallas_call x1, Pallas kernels, local(): pl.pallas_call(functools.partial(body, R, C), out_shape=(jax.ShapeDtypeSt...  208 us

profile of v1, /device:TPU:0, one launch (start us, length us, event | category | flops | bytes accessed | tf_op | source)
XLA Modules:
  0.0 213.6 jit_solution(1412046029419228757)
XLA Ops:
  0.6 207.7 %shard_map.58 = (f32[32,4096]{1,0:T(8,128)}, f32[32,4096]{1,0:T(8,128)}, f32[3,32,128]{2,1,0:T(8,128)}) custom-call(f32[4096,4096]{1,0:T(8,128)} %k_hbm.1, f32[32,4096]{1,0:T(8,128)} %src.1, f32[4,8,4096]{2,1,0:T(8,128)} %bitcast.1), custom_call_target="tpu_custom_call" | custom-call | tf_op jit(solution)/shard_map/pallas_call | solution.py:184
  208.4 0.9 reduce_sum.9
  209.2 0.6 broadcast_multiply_fusion
  209.8 1.9 copy.8
  211.7 1.9 copy.9

commit v2 on v1

--- a/solution.py
+++ b/solution.py
@@ -11,6 +11,7 @@
 BLOCK = 256
 CHUNK = 1024
 LAG = 3
+KEPT = 6
 MESH = pl.DeviceIdType.MESH
 
 
@@ -26,14 +27,18 @@
     pairs = src.shape[0]
     nb = rows // BLOCK
     pr = pairs // R
-    ring = kh.shape[0]
+    kept = min(KEPT, nb - 2)
+    ring = kh.shape[0] - kept
+
+    def home(b):
+        return jnp.where(b < kept, b, kept + lax.rem(b, ring))
+
     me_r = lax.axis_index("row")
     me_c = lax.axis_index("col")
     me_k = lax.axis_index("rep")
     other = 1 - me_k
 
     def load(b):
-        b = lax.rem(b, nb)
         return pltpu.make_async_copy(
             k_hbm.at[pl.ds(pl.multiple_of(b * BLOCK, BLOCK), BLOCK), :],
             kf.at[lax.rem(b, 2)], ksem.at[lax.rem(b, 2)])
@@ -49,8 +54,6 @@
         pl.semaphore_signal(barrier, inc=1, device_id={"row": lax.rem(me_r + k, R)}, device_id_type=MESH)
     pl.semaphore_wait(barrier, 1 + (C - 1) + (R - 1))
 
-    vhl[0:pairs, :] = jnp.ones((pairs, cols), jnp.bfloat16)
-    vhl[pairs:, :] = jnp.zeros((pairs, cols), jnp.bfloat16)
     vbuf[0, :, :, 0:cols] = jnp.ones((R, pr, cols), jnp.float32)
 
     def to_rep(src_ref, dst_ref, ssem, rsem):
@@ -79,26 +82,55 @@
         def _(s):
             @pl.when(s < nb)
             def _():
-                slot = lax.rem(s, 2)
-                hold = lax.rem(s, ring)
-                load(s).wait()
-                total = jnp.zeros((2 * pairs, BLOCK), jnp.float32)
-                for c in range(0, cols, CHUNK):
-                    hi, lo = split(kf[slot, :, c:c + CHUNK])
-                    kh[hold, :, c:c + CHUNK] = hi
-                    kl[hold, :, c:c + CHUNK] = lo
-                    v = vhl[:, c:c + CHUNK]
-                    dims = (((1,), (1,)), ((), ()))
-                    total += lax.dot_general(v, hi, dims, preferred_element_type=jnp.float32)
-                    total += lax.dot_general(v, lo, dims, preferred_element_type=jnp.float32)
-                part[base + s] = total[:pairs] + total[pairs:]
-                first(base + s).start()
-                if t < ITERS - 1:
-                    load(s + 2).start()
-                else:
+                hold = home(s)
+                fresh = (s >= kept) if t > 0 else (s >= 0)
+                dims = (((1,), (1,)), ((), ()))
+
+                @pl.when(fresh)
+                def _():
+                    slot = lax.rem(s, 2)
+                    load(s).wait()
+                    if t == 0:
+                        lanes = jnp.zeros((BLOCK, 128), jnp.float32)
+                        for c in range(0, cols, CHUNK):
+                            x = kf[slot, :, c:c + CHUNK]
+                            hi, lo = split(x)
+                            kh[hold, :, c:c + CHUNK] = hi
+                            kl[hold, :, c:c + CHUNK] = lo
+                            for d in range(0, CHUNK, 128):
+                                lanes += x[:, d:d + 128]
+                        hi, lo = split(lanes)
+                        one = jnp.ones((pairs, 128), jnp.bfloat16)
+                        part[base + s] = (lax.dot_general(one, hi, dims, preferred_element_type=jnp.float32)
+                                          + lax.dot_general(one, lo, dims, preferred_element_type=jnp.float32))
+                    else:
+                        total = jnp.zeros((2 * pairs, BLOCK), jnp.float32)
+                        for c in range(0, cols, CHUNK):
+                            hi, lo = split(kf[slot, :, c:c + CHUNK])
+                            kh[hold, :, c:c + CHUNK] = hi
+                            kl[hold, :, c:c + CHUNK] = lo
+                            v = vhl[:, c:c + CHUNK]
+                            total += lax.dot_general(v, hi, dims, preferred_element_type=jnp.float32)
+                            total += lax.dot_general(v, lo, dims, preferred_element_type=jnp.float32)
+                        part[base + s] = total[:pairs] + total[pairs:]
+
                     @pl.when(s + 2 < nb)
                     def _():
                         load(s + 2).start()
+                    if t < ITERS - 1:
+                        @pl.when(s + 2 >= nb)
+                        def _():
+                            load(s + 2 - nb + kept).start()
+
+                if t > 0:
+                    @pl.when(s < kept)
+                    def _():
+                        v = vhl[...]
+                        total = (lax.dot_general(v, kh[hold], dims, preferred_element_type=jnp.float32)
+                                 + lax.dot_general(v, kl[hold], dims, preferred_element_type=jnp.float32))
+                        part[base + s] = total[:pairs] + total[pairs:]
+
+                first(base + s).start()
 
             @pl.when((s >= 1) & (s <= nb))
             def _():
@@ -112,7 +144,7 @@
             def _():
                 b = s - LAG
                 g = base + b
-                hold = lax.rem(b, ring)
+                hold = home(b)
                 for k in range(1, C):
                     peer = lax.rem(me_c + (C - k), C)
                     to_col(k, rx2.at[g, peer], rx2.at[g, peer], s2.at[g, k], r2.at[g, k]).wait()
@@ -130,12 +162,12 @@
         for q in range(R):
             red[q] = acc[q * pr:(q + 1) * pr, :] + acc[pairs + q * pr:pairs + (q + 1) * pr, :]
         for k in range(1, R):
-            to_row(k, red.at[lax.rem(me_r + k, R)], rsrx.at[t, me_r], srs.at[k], rrs.at[k]).start()
+            to_row(k, red.at[lax.rem(me_r + k, R)], rsrx.at[me_r], srs.at[k], rrs.at[k]).start()
         total = red[me_r]
         for k in range(1, R):
             peer = lax.rem(me_r + (R - k), R)
-            to_row(k, red.at[lax.rem(me_r + k, R)], rsrx.at[t, peer], srs.at[k], rrs.at[k]).wait()
-            total += rsrx[t, peer]
+            to_row(k, red.at[lax.rem(me_r + k, R)], rsrx.at[peer], srs.at[k], rrs.at[k]).wait()
+            total += rsrx[peer]
         goal = tgt[me_r]
         diff = jnp.abs(vbuf[t, me_r, :, 0:cols] * total - goal)
         lanes = diff[:, 0:128]
@@ -180,7 +212,7 @@
     f32, bf16 = jnp.float32, jnp.bfloat16
     dma = pltpu.SemaphoreType.DMA
     vmem = pl.BlockSpec(memory_space=pltpu.VMEM)
-    ring = LAG + 1
+    ring = LAG + 1 + min(KEPT, nb - 2)
     u, v, e = pl.pallas_call(
         functools.partial(body, R, C),
         out_shape=(
@@ -197,7 +229,7 @@
             pltpu.VMEM((2 * pairs, cols), bf16),
             pltpu.VMEM((2 * pairs, cols), f32),
             pltpu.VMEM((R, pr, cols), f32),
-            pltpu.VMEM((ITERS, R, pr, cols), f32),
+            pltpu.VMEM((R, pr, cols), f32),
             pltpu.VMEM((ITERS + 1, R, pr, cols + 128), f32),
             pltpu.VMEM((2 * nb, pairs, BLOCK), f32),
             pltpu.VMEM((2 * nb, pairs, BLOCK), f32),
@@ -212,7 +244,7 @@
             dma((C,)), dma((C,)),
         ],
         compiler_params=pltpu.CompilerParams(
-            collective_id=0, has_side_effects=True, vmem_limit_bytes=60 << 20),
+            collective_id=0, has_side_effects=True, vmem_limit_bytes=62 << 20),
     )(kernel, source, target.reshape(R, pr, cols))
     return u, v, jnp.sum(e, axis=2) / (cols * D)
 

time: 215 us -> 209 us (0.972)
  Pallas kernels: 208 us -> 202 us
    pallas_call x1, Pallas kernels: 208 us -> 202 us  [local(): pl.pallas_call(functools.partial(body, R, C), out_shape=(jax.ShapeDtypeSt...]
where the time goes in v2:
time: 209 us; the launch traced here: 208 us
  Pallas kernels  202 us (97%)
  local copies, waits for them, and re-layouts  3.74 us (2%)
    pallas_call x1, Pallas kernels, local(): pl.pallas_call(functools.partial(body, R, C), out_shape=(jax.ShapeDtypeSt...  202 us

profile of v2, /device:TPU:0, one launch (start us, length us, event | category | flops | bytes accessed | tf_op | source)
XLA Modules:
  0.0 208.0 jit_solution(10640914579280916856)
XLA Ops:
  0.6 202.2 %shard_map.58 = (f32[32,4096]{1,0:T(8,128)}, f32[32,4096]{1,0:T(8,128)}, f32[3,32,128]{2,1,0:T(8,128)}) custom-call(f32[4096,4096]{1,0:T(8,128)} %k_hbm.1, f32[32,4096]{1,0:T(8,128)} %src.1, f32[4,8,4096]{2,1,0:T(8,128)} %bitcast.1), custom_call_target="tpu_custom_call" | custom-call | tf_op jit(solution)/shard_map/pallas_call | solution.py:216
  202.8 0.9 reduce_sum.9
  203.7 0.6 broadcast_multiply_fusion
  204.3 1.9 copy.8
  206.2 1.9 copy.9

commit v3 on v2

--- a/solution.py
+++ b/solution.py
@@ -93,12 +93,12 @@
                     if t == 0:
                         lanes = jnp.zeros((BLOCK, 128), jnp.float32)
                         for c in range(0, cols, CHUNK):
-                            x = kf[slot, :, c:c + CHUNK]
-                            hi, lo = split(x)
-                            kh[hold, :, c:c + CHUNK] = hi
-                            kl[hold, :, c:c + CHUNK] = lo
-                            for d in range(0, CHUNK, 128):
-                                lanes += x[:, d:d + 128]
+                            for d in range(c, c + CHUNK, 128):
+                                x = kf[slot, :, d:d + 128]
+                                hi, lo = split(x)
+                                kh[hold, :, d:d + 128] = hi
+                                kl[hold, :, d:d + 128] = lo
+                                lanes += x
                         hi, lo = split(lanes)
                         one = jnp.ones((pairs, 128), jnp.bfloat16)
                         part[base + s] = (lax.dot_general(one, hi, dims, preferred_element_type=jnp.float32)
@@ -106,12 +106,15 @@
                     else:
                         total = jnp.zeros((2 * pairs, BLOCK), jnp.float32)
                         for c in range(0, cols, CHUNK):
-                            hi, lo = split(kf[slot, :, c:c + CHUNK])
-                            kh[hold, :, c:c + CHUNK] = hi
-                            kl[hold, :, c:c + CHUNK] = lo
+                            for d in range(c, c + CHUNK, 128):
+                                hi, lo = split(kf[slot, :, d:d + 128])
+                                kh[hold, :, d:d + 128] = hi
+                                kl[hold, :, d:d + 128] = lo
                             v = vhl[:, c:c + CHUNK]
-                            total += lax.dot_general(v, hi, dims, preferred_element_type=jnp.float32)
-                            total += lax.dot_general(v, lo, dims, preferred_element_type=jnp.float32)
+                            total += lax.dot_general(v, kh[hold, :, c:c + CHUNK], dims,
+                                                     preferred_element_type=jnp.float32)
+                            total += lax.dot_general(v, kl[hold, :, c:c + CHUNK], dims,
+                                                     preferred_element_type=jnp.float32)
                         part[base + s] = total[:pairs] + total[pairs:]
 
                     @pl.when(s + 2 < nb)

time: 209 us -> 217 us (1.038)
  Pallas kernels: 202 us -> 210 us
    pallas_call x1, Pallas kernels: 202 us -> 210 us  [local(): pl.pallas_call(functools.partial(body, R, C), out_shape=(jax.ShapeDtypeSt...]
where the time goes in v3:
time: 217 us; the launch traced here: 216 us
  Pallas kernels  210 us (97%)
  local copies, waits for them, and re-layouts  3.74 us (2%)
    pallas_call x1, Pallas kernels, local(): pl.pallas_call(functools.partial(body, R, C), out_shape=(jax.ShapeDtypeSt...  210 us

profile of v3, /device:TPU:0, one launch (start us, length us, event | category | flops | bytes accessed | tf_op | source)
XLA Modules:
  0.0 216.1 jit_solution(10346258616629843793)
XLA Ops:
  0.6 210.3 %shard_map.58 = (f32[32,4096]{1,0:T(8,128)}, f32[32,4096]{1,0:T(8,128)}, f32[3,32,128]{2,1,0:T(8,128)}) custom-call(f32[4096,4096]{1,0:T(8,128)} %k_hbm.1, f32[32,4096]{1,0:T(8,128)} %src.1, f32[4,8,4096]{2,1,0:T(8,128)} %bitcast.1), custom_call_target="tpu_custom_call" | custom-call | tf_op jit(solution)/shard_map/pallas_call | solution.py:219
  210.9 0.9 reduce_sum.9
  211.8 0.6 broadcast_multiply_fusion
  212.4 1.9 copy.8
  214.3 1.9 copy.9
